TPU v7x, 256 devices: a whole 4x4x8 slice. The times are simulated.
256 devices in a mesh: row: 16 (over x, z_hi, core), col: 16 (over z_lo, y).
Axes of the slice: x: 4, y: 4, z: 8 (z_hi: 2, z_lo: 4; z = z_hi * 4 + z_lo), core: 2. Of those that a mesh axis runs over, the one named last changes fastest.
Arguments:
- diag_coords: int32 [2, 1536], replicated, may hold values from 0 to 32767
- panel_coords: int32 [2, 16, 1536], P(None, 'row', 'col'), may hold values from 0 to 32767
- test_matrix: bfloat16 [16, 1536, 512], P('row', 'col'), may hold values from -6 to 6
- ranks: int32 [16], replicated, may hold values from 64 to 512, as said below
Outputs:
- panel_left: bfloat16 [16, 1536, 512], P('row', 'col')
- update_right: bfloat16 [16, 16, 1536, 512], P('row', 'col')
Inputs may be any that keep to these rules, and one draw needn't show every extreme that they name: ranks[i] is 512 at tile 0 and 64 at the last tile and falls roughly evenly in between, with small random steps.
All inputs are finite; a program needn't handle non-finite values.
Results may differ from a plain program's by a relative error of at most 0.0068.
Values may be sent and summed in bfloat16 or wider, within the bound.
No kernel may reach another device: no remote copies, remote signals or barrier semaphores. Data moves between devices by JAX's collectives and lax.ppermute only.
A program may use at most 192 MiB of HBM per device.

v0:
```python
import jax
import jax.numpy as jnp
from jax import lax
from jax.sharding import PartitionSpec as P

range_length = 409.6
nugget = 0.5
shift_ratio = 0.01


def broadcast(value, axis, root):
    mine = lax.axis_index(axis) == root
    return lax.psum(jnp.where(mine, value, jnp.zeros_like(value)), axis)


def matern(first, second):
    delta_x = (first[0][:, None] - second[0][None, :]).astype(jnp.float32)
    delta_y = (first[1][:, None] - second[1][None, :]).astype(jnp.float32)
    return jnp.exp(-jnp.sqrt(delta_x * delta_x + delta_y * delta_y) / range_length)


def solve_right(factor, sample):
    return jax.scipy.linalg.solve_triangular(factor, sample.T, lower=True).T


def shards(diag_coords, panel_coords, test_matrix, ranks):
    points = diag_coords.shape[1]
    row_tiles = panel_coords.shape[1]
    width = test_matrix.shape[2]
    n_row = lax.axis_size("row")
    n_col = lax.axis_size("col")
    col_tiles = row_tiles * n_row // n_col
    row_index = lax.axis_index("row")
    col_index = lax.axis_index("col")
    cov = matern(diag_coords, diag_coords) + nugget * jnp.eye(points, dtype=jnp.float32)
    is_owner = (row_index == 0) & (col_index == 0)
    lower = lax.cond(is_owner, jnp.linalg.cholesky, jnp.zeros_like, cov)
    lower = broadcast(lower, ("row", "col"), 0)
    columns = jnp.arange(width, dtype=jnp.int32)
    row_ranks = lax.dynamic_slice_in_dim(ranks, row_index * row_tiles, row_tiles)
    row_mask = (columns[None, :] < row_ranks[:, None]).astype(jnp.float32)
    tests_full = lax.all_gather(test_matrix, "col", axis=1, tiled=True)
    tests_rows = tests_full * row_mask.astype(jnp.bfloat16)[:, None, :]
    local_points = panel_coords.reshape(2, -1)
    block = matern(local_points, diag_coords)
    solved = jax.scipy.linalg.solve_triangular(lower, block.T, lower=True).T
    solved = solved.reshape(row_tiles, -1, points)
    sample = jnp.einsum(
        "inm,imr->inr", solved, tests_rows.astype(jnp.float32), precision=lax.Precision.HIGHEST
    )
    gram_part = jnp.einsum("inr,ins->irs", sample, sample, precision=lax.Precision.HIGHEST)
    gram = lax.psum(gram_part, "col")
    trace = jnp.sum(jnp.diagonal(gram, axis1=1, axis2=2), axis=1)
    shift = shift_ratio * trace / row_ranks.astype(jnp.float32)
    extra = shift[:, None] * row_mask + 1.0 - row_mask
    shifted = gram + extra[:, :, None] * jnp.eye(width, dtype=jnp.float32)[None]
    factor = jnp.linalg.cholesky(shifted)
    left = jax.vmap(solve_right)(factor, sample).astype(jnp.bfloat16)
    coeff_part = jnp.einsum(
        "inm,inr->imr", solved, left.astype(jnp.float32), precision=lax.Precision.HIGHEST
    )
    coeff_piece = lax.psum_scatter(coeff_part, "col", scatter_dimension=1, tiled=True).astype(
        jnp.bfloat16
    )
    coeff = lax.all_gather(coeff_piece, "col", axis=1, tiled=True)
    left_full = lax.all_gather(left, "col", axis=1, tiled=True)
    root = col_index * col_tiles // row_tiles
    stacked = jnp.stack([left_full, coeff])
    slab = broadcast(stacked, "row", root)
    offset = col_index * col_tiles % row_tiles
    col_left = slab[0]
    col_coeff = slab[1]
    core = jnp.einsum("inr,jns->ijrs", coeff, col_coeff, preferred_element_type=jnp.float32)
    core = core.astype(jnp.bfloat16)
    update = jnp.einsum("jns,ijrs->ijnr", col_left, core, preferred_element_type=jnp.float32)
    return (left, update.astype(jnp.bfloat16))


def solution(mesh):
    in_specs = (P(), P(None, "row", "col"), P("row", "col", None), P())
    out_specs = (P("row", "col", None), P("row", "col", None, None))
    return jax.shard_map(shards, mesh=mesh, in_specs=in_specs, out_specs=out_specs, check_vma=False)
```

profile of v0, /device:TPU:24, one launch (start us, length us, event | category | flops | bytes accessed | tf_op | source)
XLA Modules:
  0.0 1680.3 jit_solution(12171304196142821972)
XLA Ops:
  8.1 0.8 slice_reduce_fusion.1
  8.9 7.0 subtract_convert_fusion
  15.9 4.3 iota.299
  20.2 4.8 triangular_solve.302
  25.0 4.8 broadcast.804
  29.8 14.6 conditional.1
  29.8 4.8 broadcast.796
  44.4 4.7 broadcast_select_fusion
  51.7 639.4 %all-reduce.6.cloned.1.call-done = f32[1536,1536]{1,0:T(8,128)} async-done(((f32[1536,1536]{1,0:T(8,128)}), f32[1536,1536]{1,0:T(8,128)}) %all-reduce.6.cloned.1.call-update) | async-done | bytes 9437200 | tf_op jit(solution)/shard_map/psum | solution.py:13
  691.1 8.4 fusion.72
  699.4 35.7 %while.2 = (s32[]{:T(128)}, f32[1536,1536]{1,0:T(8,128)}, s32[12,2]{0,1:T(2,128)S(1)}, f32[12,128,128]{2,1,0:T(8,128)S(1)}, s32[]{:T(128)}) while((s32[]{:T(128)}, f32[1536,1536]{1,0:T(8,128)}, s32[12,2]{0,1:T(2,128)S(1)}, f32[12,128,128]{2,1,0:T(8,128)S(1)}, s32[]{:T(128)}) %tuple.143), condition=%wide.while_cond, body=%wide.while_body.sunk | while | flops 2 | bytes 131181 | solution.py:46
  700.1 2.3 bitcast_dynamic-update-slice_fusion.4
  703.1 2.3 bitcast_dynamic-update-slice_fusion.4
  706.1 2.3 bitcast_dynamic-update-slice_fusion.4
  709.0 2.3 bitcast_dynamic-update-slice_fusion.4
  712.0 2.3 bitcast_dynamic-update-slice_fusion.4
  715.0 2.3 bitcast_dynamic-update-slice_fusion.4
  718.0 2.3 bitcast_dynamic-update-slice_fusion.4
  721.0 2.3 bitcast_dynamic-update-slice_fusion.4
  724.0 2.3 bitcast_dynamic-update-slice_fusion.4
  726.9 2.3 bitcast_dynamic-update-slice_fusion.4
  729.9 2.3 bitcast_dynamic-update-slice_fusion.4
  732.9 2.2 bitcast_dynamic-update-slice_fusion.4
  735.2 117.9 %custom-call.130 = f32[12,128,128]{1,2,0:T(8,128)S(1)} custom-call(f32[12,128,128]{2,1,0:T(8,128)S(1)} %get-tuple-element.41), custom_call_target="InvertDiagBlocksLowerTriangular" | custom-call | tf_op jit(solution)/shard_map/jit(_solve_triangular)/triangular_solve | solution.py:46
  853.3 1.1 convolution_subtract_fusion.11
  854.7 1.2 convolution_subtract_fusion.10
  856.2 1.3 convolution_subtract_fusion.14
  857.7 1.3 convolution_subtract_fusion.13
  859.4 1.4 convolution_subtract_fusion.12
  861.1 1.5 convolution_subtract_fusion.9
  862.8 1.6 convolution_subtract_fusion.8
  864.7 1.6 convolution_subtract_fusion.7
  866.6 1.7 convolution_subtract_fusion.6
  868.7 1.8 convolution_subtract_fusion.5
  870.7 1.9 convolution_subtract_fusion.4
  872.9 2.5 fusion.76
  875.4 2.0 convolution_bitcast_fusion.1
  878.2 157.0 %all-reduce.8.cloned.1.call-done = f32[1,512,512]{1,2,0:T(8,128)} async-done(((f32[1,512,512]{1,2,0:T(8,128)}), f32[1,512,512]{1,2,0:T(8,128)}) %all-reduce.8.cloned.1.call-update) | async-done | bytes 1048592 | tf_op jit(solution)/shard_map/psum | solution.py:52
  1035.3 8.6 gather_fusion
  1045.9 1.3 select_add_fusion.1
  1047.5 1.4 fusion.97
  1049.0 11.7 custom-call.131
  1060.8 9.8 custom-call.132
  1071.4 11.7 custom-call.133
  1083.5 10.0 custom-call.134
  1094.4 11.7 custom-call.135
  1106.3 9.8 custom-call.136
  1116.9 11.9 custom-call.137
  1128.9 0.7 compare_reduce_fusion.14
  1134.3 11.3 while.3
  1135.0 1.4 constant_dynamic-slice_fusion.8
  1137.8 1.4 constant_dynamic-slice_fusion.8
  1140.6 1.4 constant_dynamic-slice_fusion.8
  1143.4 1.4 constant_dynamic-slice_fusion.8
  1145.6 40.1 %custom-call.138 = f32[1,4,128,128]{2,3,1,0:T(8,128)S(1)} custom-call(f32[1,4,128,128]{3,2,1,0:T(8,128)} %bitcast.372), custom_call_target="InvertDiagBlocksLowerTriangular" | custom-call | tf_op jit(solution)/shard_map/vmap(jit(_solve_triangular))/triangular_solve | solution.py:23
  1187.3 4.2 convolution_bitcast_fusion
  1192.3 83.5 %reduce-scatter.2.cloned.1.call-done = f32[1,96,512]{2,1,0:T(8,128)} async-done(((f32[1,1536,512]{2,1,0:T(8,128)}), f32[1,96,512]{2,1,0:T(8,128)}) %reduce-scatter.2.cloned.1.call-update) | async-done | bytes 196624 | tf_op jit(solution)/shard_map/reduce_scatter | solution.py:62
  1275.9 1.6 convert_element_type.82
  1277.5 84.0 %all-gather.6.cloned.1.call-done = bf16[1,1536,512]{2,1,0:T(8,128)(2,1)} async-done(((bf16[1,96,512]{2,1,0:T(8,128)(2,1)}), bf16[1,1536,512]{2,1,0:T(8,128)(2,1)}) %all-gather.6.cloned.1.call-update) | async-done | bytes 1572880 | tf_op jit(solution)/shard_map/all_gather | solution.py:66
  1361.5 83.2 %all-gather.8.cloned.1.call-done = bf16[1,1536,512]{2,1,0:T(8,128)(2,1)} async-done(((bf16[1,96,512]{2,1,0:T(8,128)(2,1)}), bf16[1,1536,512]{2,1,0:T(8,128)(2,1)}) %all-gather.8.cloned.1.call-update) | async-done | bytes 1572880 | tf_op jit(solution)/shard_map/all_gather | solution.py:65
  1444.7 4.0 maximum_select_fusion
  1448.7 218.2 %all-reduce.10.cloned.1.call-done = bf16[2,1,1536,512]{3,2,1,0:T(8,128)(2,1)} async-done(((bf16[2,1,1536,512]{3,2,1,0:T(8,128)(2,1)}), bf16[2,1,1536,512]{3,2,1,0:T(8,128)(2,1)}) %all-reduce.10.cloned.1.call-update) | async-done | bytes 3145744 | tf_op jit(solution)/shard_map/psum | solution.py:13
  1666.9 3.8 fusion.73
  1670.7 1.6 copy.29
  (124 shorter events, 28.8 us)
Async XLA Ops:
  8.0 683.1 %all-reduce.6.cloned.1.call-start = ((), (), s32[]{:S(2)}) async-start(), calls=%async_computation.1 | async-start | bytes 18874368 | tf_op jit(solution)/shard_map/psum | solution.py:13
  49.1 0.7 copy-start.2
  49.1 0.7 copy-start.3
  49.1 823.8 %all-gather.4.cloned.1.call-start = ((), (), s32[]{:S(2)}) async-start(), calls=%async_computation.2 | async-start | bytes 1671168 | tf_op jit(solution)/shard_map/all_gather | solution.py:42
  49.7 985.5 %all-reduce.8.cloned.1.call-start = ((), (), s32[]{:S(2)}) async-start(), calls=%async_computation.3 | async-start | bytes 2097152 | tf_op jit(solution)/shard_map/psum | solution.py:52
  872.9 172.3 %copy-start = (f32[1536,96]{0,1:T(8,128)}, f32[1536,96]{0,1:T(8,128)S(1)}, u32[]{:S(2)}) copy-start(f32[1536,96]{0,1:T(8,128)S(1)} %convolution_dynamic-update-slice_fusion.10) | copy-start | bytes 1769476
  877.4 398.4 %reduce-scatter.2.cloned.1.call-start = ((), (), s32[]{:S(2)}) async-start(), calls=%async_computation.5 | async-start | bytes 3342336 | tf_op jit(solution)/shard_map/reduce_scatter | solution.py:62
  1191.5 170.0 %all-gather.6.cloned.1.call-start = ((), (), s32[]{:S(2)}) async-start(), calls=%async_computation.4 | async-start | bytes 1671168 | tf_op jit(solution)/shard_map/all_gather | solution.py:66
  1192.3 252.4 %all-gather.8.cloned.1.call-start = ((), (), s32[]{:S(2)}) async-start(), calls=%async_computation.6 | async-start | bytes 1671168 | tf_op jit(solution)/shard_map/all_gather | solution.py:65
  1277.5 389.4 %all-reduce.10.cloned.1.call-start = ((), (), s32[]{:S(2)}) async-start(), calls=%async_computation.7 | async-start | bytes 6291456 | tf_op jit(solution)/shard_map/psum | solution.py:13
  1444.7 222.2 %copy-start.1 = (bf16[1,1536,512]{2,1,0:T(8,128)(2,1)S(1)}, bf16[1,1536,512]{2,1,0:T(8,128)(2,1)}, u32[]{:S(2)}) copy-start(bf16[1,1536,512]{2,1,0:T(8,128)(2,1)} %all-gather.8.cloned.1.call-done) | copy-start | bytes 4718596
Sparse Core Ops, SparseCore 0:
  49.3 641.7 all-reduce.5
  1448.8 218.0 all-reduce.9
Sparse Core Ops, SparseCore 1:
  51.4 440.1 all-gather.3
  877.5 157.7 all-reduce.7
  1191.6 84.2 reduce-scatter.1
  1278.3 83.2 all-gather.5
  1363.9 80.7 all-gather.7
where the time goes:
time: 1690 us; the launch traced here: 1680 us
  waiting for transfers between devices  1270 us (75%)
  other arithmetic  269 us (16%)
  local copies, waits for them, and re-layouts  78.2 us (5%)
  matrix products  36 us (2%)
  between operations  20.7 us (1%)
    psum x2, waiting for transfers between devices, broadcast(): return lax.psum(jnp.where(mine, value, jnp.zeros_like(value)), axis)  858 us
    psum x1, waiting for transfers between devices, shards(): gram = lax.psum(gram_part, 'col')  157 us
    another operation x3, other arithmetic, shards(): solved = jax.scipy.linalg.solve_triangular(lower, block.T, lower=True).T  126 us
    all_gather x1, waiting for transfers between devices, shards(): left_full = lax.all_gather(left, 'col', axis=1, tiled=True)  84 us
    reduce_scatter x1, waiting for transfers between devices, shards(): lax.psum_scatter(coeff_part, 'col', scatter_dimension=1, tiled=True)  83.5 us
    all_gather x1, waiting for transfers between devices, shards(): coeff = lax.all_gather(coeff_piece, 'col', axis=1, tiled=True)  83.2 us
    another operation x15, other arithmetic, shards(): factor = jnp.linalg.cholesky(shifted)  79.4 us
    another operation x58, local copies, waits for them, and re-layouts  56.4 us
  transfers between devices with their start and end apart: 7, of which 6 were waited for; matrix products, arithmetic and copies ran while one was open for 11% of the time, Pallas kernels for 0%

commit v1 on v0

--- a/solution.py
+++ b/solution.py
@@ -62,8 +62,11 @@
     coeff_piece = lax.psum_scatter(coeff_part, "col", scatter_dimension=1, tiled=True).astype(
         jnp.bfloat16
     )
-    coeff = lax.all_gather(coeff_piece, "col", axis=1, tiled=True)
-    left_full = lax.all_gather(left, "col", axis=1, tiled=True)
+    coeff, left_full = jnp.split(
+        lax.all_gather(jnp.concatenate([coeff_piece, left], axis=0), "col", axis=1, tiled=True),
+        [coeff_piece.shape[0]],
+        axis=0,
+    )
     root = col_index * col_tiles // row_tiles
     stacked = jnp.stack([left_full, coeff])
     slab = broadcast(stacked, "row", root)

time: 1690 us -> 1610 us (0.953)
  waiting for transfers between devices: 1270 us -> 1190 us
    all_gather x2 -> x1, waiting for transfers between devices: 167 us -> 87.8 us  [shards(): lax.all_gather(jnp.concatenate([coeff_piece, left], axis=0), 'col', axis=...]
    another operation x58 -> x59, local copies, waits for them, and re-layouts: 56.4 us -> 58.6 us
  transfers between devices with their start and end apart: 7 -> 6, of which waited for: 6 -> 5; matrix products, arithmetic and copies ran while one was open for 11% -> 11% of each run, Pallas kernels for 0% -> 0%
where the time goes in v1:
time: 1610 us; the launch traced here: 1600 us
  waiting for transfers between devices  1190 us (74%)
  other arithmetic  267 us (17%)
  local copies, waits for them, and re-layouts  81.5 us (5%)
  matrix products  37.2 us (2%)
  between operations  20.7 us (1%)
    psum x2, waiting for transfers between devices, broadcast(): return lax.psum(jnp.where(mine, value, jnp.zeros_like(value)), axis)  859 us
    psum x1, waiting for transfers between devices, shards(): gram = lax.psum(gram_part, 'col')  157 us
    another operation x3, other arithmetic, shards(): solved = jax.scipy.linalg.solve_triangular(lower, block.T, lower=True).T  126 us
    all_gather x1, waiting for transfers between devices, shards(): lax.all_gather(jnp.concatenate([coeff_piece, left], axis=0), 'col', axis=...  87.8 us
    reduce_scatter x1, waiting for transfers between devices, shards(): lax.psum_scatter(coeff_part, 'col', scatter_dimension=1, tiled=True)  84.3 us
    another operation x15, other arithmetic, shards(): factor = jnp.linalg.cholesky(shifted)  79.4 us
    another operation x58, local copies, waits for them, and re-layouts  56.4 us
    another operation x3, other arithmetic, solve_right(): return jax.scipy.linalg.solve_triangular(factor, sample.T, lower=True).T  40.3 us
  transfers between devices with their start and end apart: 6, of which 5 were waited for; matrix products, arithmetic and copies ran while one was open for 11% of the time, Pallas kernels for 0%

profile of v1, /device:TPU:24, one launch (start us, length us, event | category | flops | bytes accessed | tf_op | source)
XLA Modules:
  0.0 1604.7 jit_solution(934094754466460791)
XLA Ops:
  8.1 0.8 slice_reduce_fusion.1
  8.9 7.0 subtract_convert_fusion
  15.9 4.3 iota.299
  20.2 4.8 triangular_solve.302
  25.0 4.8 broadcast.804
  29.8 14.6 conditional.1
  29.8 4.8 broadcast.796
  44.4 4.7 broadcast_select_fusion
  51.7 639.4 %all-reduce.6.cloned.1.call-done = f32[1536,1536]{1,0:T(8,128)} async-done(((f32[1536,1536]{1,0:T(8,128)}), f32[1536,1536]{1,0:T(8,128)}) %all-reduce.6.cloned.1.call-update) | async-done | bytes 9437200 | tf_op jit(solution)/shard_map/psum | solution.py:13
  691.1 8.4 fusion.72
  699.4 35.7 %while.2 = (s32[]{:T(128)}, f32[1536,1536]{1,0:T(8,128)}, s32[12,2]{0,1:T(2,128)S(1)}, f32[12,128,128]{2,1,0:T(8,128)S(1)}, s32[]{:T(128)}) while((s32[]{:T(128)}, f32[1536,1536]{1,0:T(8,128)}, s32[12,2]{0,1:T(2,128)S(1)}, f32[12,128,128]{2,1,0:T(8,128)S(1)}, s32[]{:T(128)}) %tuple.144), condition=%wide.while_cond, body=%wide.while_body.sunk | while | flops 2 | bytes 131181 | solution.py:46
  700.1 2.3 bitcast_dynamic-update-slice_fusion.4
  703.1 2.3 bitcast_dynamic-update-slice_fusion.4
  706.1 2.3 bitcast_dynamic-update-slice_fusion.4
  709.0 2.3 bitcast_dynamic-update-slice_fusion.4
  712.0 2.3 bitcast_dynamic-update-slice_fusion.4
  715.0 2.3 bitcast_dynamic-update-slice_fusion.4
  718.0 2.3 bitcast_dynamic-update-slice_fusion.4
  721.0 2.3 bitcast_dynamic-update-slice_fusion.4
  724.0 2.3 bitcast_dynamic-update-slice_fusion.4
  726.9 2.3 bitcast_dynamic-update-slice_fusion.4
  729.9 2.3 bitcast_dynamic-update-slice_fusion.4
  732.9 2.2 bitcast_dynamic-update-slice_fusion.4
  735.2 117.9 %custom-call.130 = f32[12,128,128]{1,2,0:T(8,128)S(1)} custom-call(f32[12,128,128]{2,1,0:T(8,128)S(1)} %get-tuple-element.41), custom_call_target="InvertDiagBlocksLowerTriangular" | custom-call | tf_op jit(solution)/shard_map/jit(_solve_triangular)/triangular_solve | solution.py:46
  853.3 1.1 convolution_subtract_fusion.11
  854.7 1.2 convolution_subtract_fusion.10
  856.2 1.3 convolution_subtract_fusion.14
  857.7 1.3 convolution_subtract_fusion.13
  859.4 1.4 convolution_subtract_fusion.12
  861.1 1.5 convolution_subtract_fusion.9
  862.8 1.6 convolution_subtract_fusion.8
  864.7 1.6 convolution_subtract_fusion.7
  866.6 1.7 convolution_subtract_fusion.6
  868.7 1.8 convolution_subtract_fusion.5
  870.7 1.9 convolution_subtract_fusion.4
  872.9 2.5 fusion.76
  875.4 2.0 convolution_bitcast_fusion.1
  878.2 157.0 %all-reduce.8.cloned.1.call-done = f32[1,512,512]{1,2,0:T(8,128)} async-done(((f32[1,512,512]{1,2,0:T(8,128)}), f32[1,512,512]{1,2,0:T(8,128)}) %all-reduce.8.cloned.1.call-update) | async-done | bytes 1048592 | tf_op jit(solution)/shard_map/psum | solution.py:52
  1035.3 8.6 gather_fusion
  1045.9 1.3 select_add_fusion.1
  1047.5 1.4 fusion.98
  1049.0 11.7 custom-call.131
  1060.8 9.8 custom-call.132
  1071.4 11.7 custom-call.133
  1083.5 10.0 custom-call.134
  1094.4 11.7 custom-call.135
  1106.3 9.8 custom-call.136
  1116.9 11.9 custom-call.137
  1128.9 0.7 compare_reduce_fusion.14
  1134.3 11.3 while.3
  1135.0 1.4 constant_dynamic-slice_fusion.8
  1137.8 1.4 constant_dynamic-slice_fusion.8
  1140.6 1.4 constant_dynamic-slice_fusion.8
  1143.4 1.4 constant_dynamic-slice_fusion.8
  1145.6 40.1 %custom-call.138 = f32[1,4,128,128]{2,3,1,0:T(8,128)S(1)} custom-call(f32[1,4,128,128]{3,2,1,0:T(8,128)} %bitcast.372), custom_call_target="InvertDiagBlocksLowerTriangular" | custom-call | tf_op jit(solution)/shard_map/vmap(jit(_solve_triangular))/triangular_solve | solution.py:23
  1187.3 4.2 convolution_bitcast_fusion
  1191.6 84.3 %reduce-scatter.2.cloned.1.call-done = f32[1,96,512]{2,1,0:T(8,128)} async-done(((f32[1,1536,512]{2,1,0:T(8,128)}), f32[1,96,512]{2,1,0:T(8,128)}) %reduce-scatter.2.cloned.1.call-update) | async-done | bytes 196624 | tf_op jit(solution)/shard_map/reduce_scatter | solution.py:62
  1275.9 0.9 convert_element_type.82
  1277.6 87.8 %all-gather.5.cloned.1.call-done = bf16[2,1536,512]{2,1,0:T(8,128)(2,1)} async-done(((bf16[2,96,512]{2,1,0:T(8,128)(2,1)}), bf16[2,1536,512]{2,1,0:T(8,128)(2,1)}) %all-gather.5.cloned.1.call-update) | async-done | bytes 3145744 | tf_op jit(solution)/shard_map/all_gather | solution.py:66
  1365.4 2.2 slice_bitcast_fusion.4
  1367.6 2.0 maximum_select_fusion
  1369.7 219.4 %all-reduce.10.cloned.1.call-done = bf16[2,1,1536,512]{3,2,1,0:T(8,128)(2,1)} async-done(((bf16[2,1,1536,512]{3,2,1,0:T(8,128)(2,1)}), bf16[2,1,1536,512]{3,2,1,0:T(8,128)(2,1)}) %all-reduce.10.cloned.1.call-update) | async-done | bytes 3145744 | tf_op jit(solution)/shard_map/psum | solution.py:13
  1589.1 5.0 fusion.73
  1594.1 2.6 copy.29
  (125 shorter events, 28.8 us)
Async XLA Ops:
  8.0 683.1 %all-reduce.6.cloned.1.call-start = ((), (), s32[]{:S(2)}) async-start(), calls=%async_computation.1 | async-start | bytes 18874368 | tf_op jit(solution)/shard_map/psum | solution.py:13
  49.1 0.7 copy-start.3
  49.1 0.7 copy-start.4
  49.1 823.8 %all-gather.3.cloned.1.call-start = ((), (), s32[]{:S(2)}) async-start(), calls=%async_computation.2 | async-start | bytes 1671168 | tf_op jit(solution)/shard_map/all_gather | solution.py:42
  49.7 985.5 %all-reduce.8.cloned.1.call-start = ((), (), s32[]{:S(2)}) async-start(), calls=%async_computation.3 | async-start | bytes 2097152 | tf_op jit(solution)/shard_map/psum | solution.py:52
  872.9 172.3 %copy-start.1 = (f32[1536,96]{0,1:T(8,128)}, f32[1536,96]{0,1:T(8,128)S(1)}, u32[]{:S(2)}) copy-start(f32[1536,96]{0,1:T(8,128)S(1)} %convolution_dynamic-update-slice_fusion.10) | copy-start | bytes 1769476
  877.4 398.4 %reduce-scatter.2.cloned.1.call-start = ((), (), s32[]{:S(2)}) async-start(), calls=%async_computation.4 | async-start | bytes 3342336 | tf_op jit(solution)/shard_map/reduce_scatter | solution.py:62
  1191.5 173.8 %all-gather.5.cloned.1.call-start = ((), (), s32[]{:S(2)}) async-start(), calls=%async_computation.5 | async-start | bytes 3342336 | tf_op jit(solution)/shard_map/all_gather | solution.py:66
  1191.6 402.5 %copy-start.2 = (bf16[1,96,512]{2,1,0:T(8,128)(2,1)}, bf16[1,96,512]{2,1,0:T(8,128)(2,1)S(1)}, u32[]{:S(2)}) copy-start(bf16[1,96,512]{2,1,0:T(8,128)(2,1)S(1)} %fusion.152) | copy-start | bytes 294916
  1277.5 311.5 %all-reduce.10.cloned.1.call-start = ((), (), s32[]{:S(2)}) async-start(), calls=%async_computation.6 | async-start | bytes 6291456 | tf_op jit(solution)/shard_map/psum | solution.py:13
  1365.4 223.7 %copy-start = (bf16[2,1536,512]{2,1,0:T(8,128)(2,1)S(1)}, bf16[2,1536,512]{2,1,0:T(8,128)(2,1)}, u32[]{:S(2)}) copy-start(bf16[2,1536,512]{2,1,0:T(8,128)(2,1)} %all-gather.5.cloned.1.call-done) | copy-start | bytes 9437188
Sparse Core Ops, SparseCore 0:
  49.3 641.7 all-reduce.5
  1369.8 219.2 all-reduce.9
Sparse Core Ops, SparseCore 1:
  51.4 440.1 all-gather.2
  877.5 157.7 all-reduce.7
  1191.6 84.2 reduce-scatter.1
  1278.3 87.0 all-gather.4
